TPU v7x, 256 devices: a whole 4x4x8 slice. The times are simulated.
256 devices in a mesh: lat: 16 (over x_lo, z), lon: 16 (over y, x_hi, core).
Axes of the slice: x: 4 (x_hi: 2, x_lo: 2; x = x_hi * 2 + x_lo), y: 4, z: 8, core: 2. Of those that a mesh axis runs over, the one named last changes fastest.
Arguments:
- field_in: bfloat16 [160, 1536, 512], P('lat', 'lon'), may hold values from -6 to 6
- kernel_taps: bfloat16 [3, 160, 3, 33], P(None, 'lat'), may hold values from -0.8984375 to 0.8984375
- row_reach: int32 [160], P('lat'), may hold values from 1 to 16, as said below
- mix_weight: bfloat16 [3, 512, 512], replicated, may hold values from -0.15625 to 0.15625
- up_weight: bfloat16 [512, 1024], replicated, may hold values from -0.25 to 0.25
- down_weight: bfloat16 [1024, 512], replicated, may hold values from -0.1875 to 0.1875
- cotangent: bfloat16 [160, 1536, 512], P('lat', 'lon'), may hold values from -6 to 6
Outputs:
- block_out: bfloat16 [160, 1536, 512], P('lat', 'lon')
- grad_field: bfloat16 [160, 1536, 512], P('lat', 'lon')
- grad_mix: bfloat16 [3, 512, 512], replicated
- grad_up: bfloat16 [512, 1024], replicated
- grad_down: bfloat16 [1024, 512], replicated
Inputs may be any that keep to these rules, and one draw needn't show every extreme that they name: `row_reach`: how many longitude cells each latitude row's kernel reaches on either side.
All inputs are finite; a program needn't handle non-finite values.
Results may differ from a plain program's by a relative error of at most 0.0068.
Values may be sent and summed in bfloat16 or wider, within the bound.
A program may use at most 128 MiB of HBM per device.

v0:
```python
import math
import jax
import jax.numpy as jnp
from jax import lax
from jax.sharding import PartitionSpec as P

inv_root_two = 0.7071067811865476
inv_root_tau = 0.3989422804014327


def extended_2(x, sides, width, wrap):
    for axis, dim in sides:
        devices, length = (lax.axis_size(axis), x.shape[dim])
        up = [(i, (i + 1) % devices) for i in range(devices if wrap else devices - 1)]
        down = [(j, i) for i, j in up]
        last = lax.slice_in_dim(x, length - width, length, axis=dim)
        leading = lax.slice_in_dim(x, 0, width, axis=dim)
        before = lax.ppermute(last, axis, up)
        after = lax.ppermute(leading, axis, down)
        x = jnp.concatenate([before, x, after], axis=dim)
    return x


def shifted(block, axis, distance):
    devices = range(lax.axis_size(axis))
    route = [((i - distance) % len(devices), i) for i in devices]
    return lax.ppermute(block, axis, route)


def gelu_exact(value):
    return 0.5 * value * (1.0 + jax.scipy.special.erf(value * inv_root_two))


def gelu_slope(value):
    return (
        0.5 * (1.0 + jax.scipy.special.erf(value * inv_root_two))
        + value * jnp.exp(-0.5 * value * value) * inv_root_tau
    )


def local(field_in, kernel_taps, row_reach, mix_weight, up_weight, down_weight, cotangent):
    lat_rows, lon_cols, channels = field_in.shape
    basis_count = kernel_taps.shape[0]
    tap_count = kernel_taps.shape[3]
    reach_cells = (tap_count - 1) // 2
    lat_count = lax.axis_size("lat")
    lon_count = lax.axis_size("lon")
    lat_place = lax.axis_index("lat")
    north_pole = lat_place == 0
    south_pole = lat_place == lat_count - 1
    first_pass = extended_2(field_in, (("lat", 0),), 1, False)
    extended = extended_2(first_pass, (("lon", 1),), reach_cells, True)
    across = shifted(jnp.stack([extended[1], extended[lat_rows]]), "lon", lon_count // 2)
    extended = extended.at[0].set(jnp.where(north_pole, across[0], extended[0]))
    extended = extended.at[lat_rows + 1].set(
        jnp.where(south_pole, across[1], extended[lat_rows + 1])
    )
    padded_width = lon_cols + 2 * reach_cells
    offsets = jnp.arange(tap_count, dtype=jnp.int32) - reach_cells
    tap_mask = jnp.abs(offsets)[None, :] <= row_reach[:, None]
    masked_taps = jnp.where(
        tap_mask[None, :, None, :], kernel_taps, jnp.zeros((), kernel_taps.dtype)
    )
    selector = (
        jnp.arange(padded_width, dtype=jnp.int32)[None, :, None]
        - jnp.arange(lon_cols, dtype=jnp.int32)[:, None, None]
        == jnp.arange(tap_count, dtype=jnp.int32)[None, None, :]
    ).astype(jnp.bfloat16)
    band_matrix = jnp.einsum(
        "krdt,jat->krjda", masked_taps, selector, preferred_element_type=jnp.float32
    ).astype(jnp.bfloat16)
    windows = jnp.stack(
        [extended[0:lat_rows], extended[1 : lat_rows + 1], extended[2 : lat_rows + 2]], axis=1
    )
    features = jnp.einsum(
        "krjda,rdac->krjc", band_matrix, windows, preferred_element_type=jnp.float32
    ).astype(jnp.bfloat16)
    points = lat_rows * lon_cols
    flat_features = features.reshape(basis_count, points, channels)
    flat_field = field_in.reshape(points, channels)
    conv_sum = jnp.einsum(
        "kpc,kcd->pd", flat_features, mix_weight, preferred_element_type=jnp.float32
    )
    hidden = (flat_field.astype(jnp.float32) + conv_sum).astype(jnp.bfloat16)
    pre_act = jnp.dot(hidden, up_weight, preferred_element_type=jnp.float32)
    activated = gelu_exact(pre_act).astype(jnp.bfloat16)
    block_out = (
        hidden.astype(jnp.float32)
        + jnp.dot(activated, down_weight, preferred_element_type=jnp.float32)
    ).astype(jnp.bfloat16)
    grad_rows = cotangent.reshape(points, channels)
    act_grad = lax.dot_general(
        grad_rows, down_weight, (((1,), (1,)), ((), ())), preferred_element_type=jnp.float32
    )
    pre_grad = (act_grad * gelu_slope(pre_act)).astype(jnp.bfloat16)
    down_local = lax.dot_general(
        activated, grad_rows, (((0,), (0,)), ((), ())), preferred_element_type=jnp.float32
    )
    up_local = lax.dot_general(
        hidden, pre_grad, (((0,), (0,)), ((), ())), preferred_element_type=jnp.float32
    )
    hidden_grad = (
        grad_rows.astype(jnp.float32)
        + lax.dot_general(
            pre_grad, up_weight, (((1,), (1,)), ((), ())), preferred_element_type=jnp.float32
        )
    ).astype(jnp.bfloat16)
    mix_local = jnp.einsum(
        "kpc,pd->kcd", flat_features, hidden_grad, preferred_element_type=jnp.float32
    )
    feat_grad = jnp.einsum(
        "pd,kcd->kpc", hidden_grad, mix_weight, preferred_element_type=jnp.float32
    ).astype(jnp.bfloat16)
    feat_grad_rows = feat_grad.reshape(basis_count, lat_rows, lon_cols, channels)
    spread = jnp.einsum(
        "krjda,krjc->rdac", band_matrix, feat_grad_rows, preferred_element_type=jnp.float32
    )
    pulled = (
        jnp.pad(spread[:, 0], ((0, 2), (0, 0), (0, 0)))
        + jnp.pad(spread[:, 1], ((1, 1), (0, 0), (0, 0)))
        + jnp.pad(spread[:, 2], ((2, 0), (0, 0), (0, 0)))
    )
    returned = shifted(
        jnp.stack([pulled[0], pulled[lat_rows + 1]]).astype(jnp.bfloat16), "lon", lon_count // 2
    ).astype(jnp.float32)
    pulled = pulled.at[1].add(jnp.where(north_pole, returned[0], jnp.zeros_like(returned[0])))
    pulled = pulled.at[lat_rows].add(
        jnp.where(south_pole, returned[1], jnp.zeros_like(returned[1]))
    )
    col_rims = jnp.concatenate(
        [pulled[:, :reach_cells], pulled[:, lon_cols + reach_cells :]], axis=1
    )
    col_edges = extended_2(col_rims.astype(jnp.bfloat16), (("lon", 1),), reach_cells, True).astype(
        col_rims.dtype
    )
    interior = pulled[:, reach_cells : reach_cells + lon_cols]
    interior = interior.at[:, :reach_cells].add(col_edges[:, :reach_cells])
    interior = interior.at[:, lon_cols - reach_cells :].add(col_edges[:, 3 * reach_cells :])
    row_edges = extended_2(
        jnp.stack([interior[0], interior[lat_rows + 1]]).astype(jnp.bfloat16),
        (("lat", 0),),
        1,
        False,
    ).astype(jnp.float32)
    adjoint = interior[1 : lat_rows + 1]
    adjoint = adjoint.at[0].add(row_edges[0])
    adjoint = adjoint.at[lat_rows - 1].add(row_edges[3])
    grad_field = (
        hidden_grad.astype(jnp.float32).reshape(lat_rows, lon_cols, channels) + adjoint
    ).astype(jnp.bfloat16)
    grad_scale = 1.0 / math.sqrt(points * lat_count * lon_count)
    mix_total, up_total, down_total = lax.psum((mix_local, up_local, down_local), ("lat", "lon"))
    mix_out = (mix_total * grad_scale).astype(jnp.bfloat16)
    up_out = (up_total * grad_scale).astype(jnp.bfloat16)
    down_out = (down_total * grad_scale).astype(jnp.bfloat16)
    return (block_out.reshape(lat_rows, lon_cols, channels), grad_field, mix_out, up_out, down_out)


def solution(mesh):
    placed = (
        P("lat", "lon", None),
        P(None, "lat", None, None),
        P("lat"),
        P(),
        P(),
        P(),
        P("lat", "lon", None),
    )
    return jax.shard_map(
        local,
        mesh=mesh,
        in_specs=placed,
        out_specs=(P("lat", "lon", None), P("lat", "lon", None), P(), P(), P()),
        check_vma=False,
    )
```

profile of v0, /device:TPU:8, one launch (start us, length us, event | category | flops | bytes accessed | tf_op | source)
XLA Modules:
  0.0 365.4 jit_solution(5280903188768959156)
XLA Ops:
  9.6 4.6 %collective-permute-start = (bf16[1,96,512]{2,1,0:T(8,128)(2,1)S(1)}, bf16[1,96,512]{2,1,0:T(8,128)(2,1)S(1)}, u32[]{:S(2)}, u32[]{:S(2)}) collective-permute-start(bf16[1,96,512]{2,1,0:T(8,128)(2,1)S(1)} %get-tuple-element.123), channel_id=1, source_target_pairs={{0,16},{16,32},{32,48},{48,64},{64,80},{80,96},{96,112},{112,128},... | collective-permute-start | bytes 294920 | tf_op jit(solution)/shard_map/ppermute | solution.py:18
  17.8 4.1 %collective-permute-start.3 = (bf16[12,16,512]{2,1,0:T(8,128)(2,1)S(1)}, bf16[12,16,512]{2,1,0:T(8,128)(2,1)S(1)}, u32[]{:S(2)}, u32[]{:S(2)}) collective-permute-start(bf16[12,16,512]{2,1,0:T(8,128)(2,1)S(1)} %get-tuple-element.121), channel_id=1, source_target_pairs={{1,0},{2,1},{3,2},{4,3},{5,4},{6,5},{7,6},{8,7},{9,8},{10,9},{11,1... | collective-permute-start | bytes 589832 | tf_op jit(solution)/shard_map/ppermute | solution.py:19
  22.0 6.0 %collective-permute-done.2 = bf16[12,16,512]{2,1,0:T(8,128)(2,1)S(1)} collective-permute-done((bf16[12,16,512]{2,1,0:T(8,128)(2,1)S(1)}, bf16[12,16,512]{2,1,0:T(8,128)(2,1)S(1)}, u32[]{:S(2)}, u32[]{:S(2)}) %collective-permute-start.2) | collective-permute-done | bytes 196640 | tf_op jit(solution)/shard_map/ppermute | solution.py:18
  28.2 2.1 collective-permute-start.4
  31.4 7.1 %collective-permute-done.4 = bf16[2,128,512]{2,1,0:T(8,128)(2,1)S(1)} collective-permute-done((bf16[2,128,512]{2,1,0:T(8,128)(2,1)S(1)}, bf16[2,128,512]{2,1,0:T(8,128)(2,1)S(1)}, u32[]{:S(2)}, u32[]{:S(2)}) %collective-permute-start.4) | collective-permute-done | bytes 262176 | tf_op jit(solution)/shard_map/ppermute | solution.py:27
  39.1 1.9 fusion.11
  42.2 1.7 fusion.19
  44.0 4.1 %multiply_convert_fusion = (bf16[960,1024]{1,0:T(8,128)(2,1)S(1)}, f32[960,1024]{1,0:T(8,128)S(1)}) fusion(bf16[960,512]{1,0:T(8,128)(2,1)S(1)} %fusion.19, bf16[512,1024]{1,0:T(8,128)(2,1)S(1)} %copy-done.12), kind=kOutput, calls=%fused_computation.14 | convolution fusion | flops 1011548160 | bytes 7929856 | tf_op jit(solution)/shard_map/dot_general | solution.py:85
  48.2 2.5 fusion.5
  51.9 2.6 fusion.46
  54.5 3.5 fusion.22
  58.0 3.3 convolution_convert_fusion
  61.4 2.7 fusion.47
  64.0 4.1 %convolution_bitcast_fusion = f32[10,3,128,512]{3,2,0,1:T(8,128)S(1)} fusion(bf16[3,10,96,512]{3,2,1,0:T(8,128)(2,1)} %bitcast.83, bf16[3,10,96,3,128]{4,1,3,0,2:T(8,128)(2,1)S(1)} %copy-done.3), kind=kOutput, calls=%fused_computation.19 | convolution fusion | flops 1132462080 | bytes 13025280 | tf_op jit(solution)/shard_map/krjda,krjc->rdac/dot_general | solution.py:115
  68.1 3.7 %slice_bitcast_fusion.2 = (f32[10,128,512]{2,1,0:T(8,128)S(1)}, f32[10,128,512]{2,1,0:T(8,128)}, f32[10,128,512]{2,1,0:T(8,128)}) fusion(f32[10,3,128,512]{3,2,0,1:T(8,128)S(1)} %convolution_bitcast_fusion), kind=kLoop, calls=%fused_computation.25 | loop fusion | bytes 15728640 | tf_op jit(solution)/shard_map/squeeze | solution.py:119
  71.9 3.7 %fusion.39 = (bf16[12,128,512]{2,1,0:T(8,128)(2,1)S(1)}, f32[12,128,512]{2,1,0:T(8,128)S(1)}) fusion(f32[10,128,512]{2,1,0:T(8,128)} %get-tuple-element.108, f32[10,128,512]{2,1,0:T(8,128)} %get-tuple-element.107, f32[10,128,512]{2,1,0:T(8,128)S(1)} %get-tuple-element.106), kind=kLoop, calls=%fused_computation.83 | loop fusion | flops 2359296 | bytes 12582912 | tf_op jit(solution)/shard_map/convert.13
  76.9 8.7 %collective-permute-done.5 = bf16[2,128,512]{2,1,0:T(8,128)(2,1)S(1)} collective-permute-done((bf16[2,128,512]{2,1,0:T(8,128)(2,1)S(1)}, bf16[2,128,512]{2,1,0:T(8,128)(2,1)S(1)}, u32[]{:S(2)}, u32[]{:S(2)}) %collective-permute-start.5) | collective-permute-done | bytes 262176 | tf_op jit(solution)/shard_map/ppermute | solution.py:27
  86.2 4.1 %collective-permute-start.7 = (bf16[12,16,512]{2,1,0:T(8,128)(2,1)S(1)}, bf16[12,16,512]{2,1,0:T(8,128)(2,1)S(1)}, u32[]{:S(2)}, u32[]{:S(2)}) collective-permute-start(bf16[12,16,512]{2,1,0:T(8,128)(2,1)S(1)} %get-tuple-element.110), channel_id=1, source_target_pairs={{1,0},{2,1},{3,2},{4,3},{5,4},{6,5},{7,6},{8,7},{9,8},{10,9},{11,1... | collective-permute-start | bytes 589832 | tf_op jit(solution)/shard_map/ppermute | solution.py:19
  90.6 4.2 %collective-permute-done.6 = bf16[12,16,512]{2,1,0:T(8,128)(2,1)S(1)} collective-permute-done((bf16[12,16,512]{2,1,0:T(8,128)(2,1)S(1)}, bf16[12,16,512]{2,1,0:T(8,128)(2,1)S(1)}, u32[]{:S(2)}, u32[]{:S(2)}) %collective-permute-start.6) | collective-permute-done | bytes 196640 | tf_op jit(solution)/shard_map/ppermute | solution.py:18
  95.2 4.0 %collective-permute-start.8 = (bf16[1,96,512]{2,1,0:T(8,128)(2,1)S(1)}, bf16[1,96,512]{2,1,0:T(8,128)(2,1)S(1)}, u32[]{:S(2)}, u32[]{:S(2)}) collective-permute-start(bf16[1,96,512]{2,1,0:T(8,128)(2,1)S(1)} %get-tuple-element.118), channel_id=1, source_target_pairs={{0,16},{16,32},{32,48},{48,64},{64,80},{80,96},{96,112},{112,128},... | collective-permute-start | bytes 294920 | tf_op jit(solution)/shard_map/ppermute | solution.py:18
  100.5 2.1 add_convert_fusion.1
  102.8 4.0 %collective-permute-done.9 = bf16[1,96,512]{2,1,0:T(8,128)(2,1)S(1)} collective-permute-done((bf16[1,96,512]{2,1,0:T(8,128)(2,1)S(1)}, bf16[1,96,512]{2,1,0:T(8,128)(2,1)S(1)}, u32[]{:S(2)}, u32[]{:S(2)}) %collective-permute-start.9) | collective-permute-done | bytes 98336 | tf_op jit(solution)/shard_map/ppermute | solution.py:19
  108.2 243.5 %all-reduce.6.cloned.1.call-done = (f32[3,512,512]{2,1,0:T(8,128)}, f32[512,1024]{1,0:T(8,128)}, f32[1024,512]{1,0:T(8,128)}) async-done(((f32[3,512,512]{2,1,0:T(8,128)}, f32[512,1024]{1,0:T(8,128)}, f32[1024,512]{1,0:T(8,128)}), (f32[3,512,512]{2,1,0:T(8,128)}, f32[512,1024]{1,0:T(8,128)}, f32[1024,512]{1,0:T(8,128)})) %all-reduce.6.cloned.1.call-update) | async-done | bytes 7340048 | tf_op jit(solution)/shard_map/psum | solution.py:152
  351.7 3.6 multiply_convert_fusion.1
  (84 shorter events, 18.8 us)
Async XLA Ops:
  7.2 34.1 %copy-start = (bf16[3,512,512]{2,1,0:T(8,128)(2,1)S(1)}, bf16[3,512,512]{2,1,0:T(8,128)(2,1)}, u32[]{:S(2)}) copy-start(bf16[3,512,512]{2,1,0:T(8,128)(2,1)} %param.26) | copy-start | bytes 4718596
  7.2 14.8 %copy-start.11 = (bf16[3,10,3,33]{3,2,1,0:T(4,128)(2,1)S(1)}, bf16[3,10,3,33]{3,2,1,0:T(4,128)(2,1)}, u32[]{:S(2)}) copy-start(bf16[3,10,3,33]{3,2,1,0:T(4,128)(2,1)} %param.24) | copy-start | bytes 17824
  7.2 344.5 %all-reduce.6.cloned.1.call-start = ((), (), s32[]{:S(2)}) async-start(), calls=%async_computation | async-start | bytes 14680064 | tf_op jit(solution)/shard_map/psum | solution.py:152
  8.3 9.4 %collective-permute-start.1 = (bf16[1,96,512]{2,1,0:T(8,128)(2,1)S(1)}, bf16[1,96,512]{2,1,0:T(8,128)(2,1)S(1)}, u32[]{:S(2)}, u32[]{:S(2)}) collective-permute-start(bf16[1,96,512]{2,1,0:T(8,128)(2,1)S(1)} %get-tuple-element.122), channel_id=1, source_target_pairs={{16,0},{32,16},{48,32},{64,48},{80,64},{96,80},{112,96},{128,112},... | collective-permute-start | bytes 294920 | tf_op jit(solution)/shard_map/ppermute | solution.py:19
  9.6 6.8 %collective-permute-start = (bf16[1,96,512]{2,1,0:T(8,128)(2,1)S(1)}, bf16[1,96,512]{2,1,0:T(8,128)(2,1)S(1)}, u32[]{:S(2)}, u32[]{:S(2)}) collective-permute-start(bf16[1,96,512]{2,1,0:T(8,128)(2,1)S(1)} %get-tuple-element.123), channel_id=1, source_target_pairs={{0,16},{16,32},{32,48},{48,64},{64,80},{80,96},{96,112},{112,128},... | collective-permute-start | bytes 294920 | tf_op jit(solution)/shard_map/ppermute | solution.py:18
  17.7 10.2 %collective-permute-start.2 = (bf16[12,16,512]{2,1,0:T(8,128)(2,1)S(1)}, bf16[12,16,512]{2,1,0:T(8,128)(2,1)S(1)}, u32[]{:S(2)}, u32[]{:S(2)}) collective-permute-start(bf16[12,16,512]{2,1,0:T(8,128)(2,1)S(1)} %get-tuple-element.120), channel_id=1, source_target_pairs={{0,1},{1,2},{2,3},{3,4},{4,5},{5,6},{6,7},{7,8},{8,9},{9,10},{10,1... | collective-permute-start | bytes 589832 | tf_op jit(solution)/shard_map/ppermute | solution.py:18
  17.8 10.2 %collective-permute-start.3 = (bf16[12,16,512]{2,1,0:T(8,128)(2,1)S(1)}, bf16[12,16,512]{2,1,0:T(8,128)(2,1)S(1)}, u32[]{:S(2)}, u32[]{:S(2)}) collective-permute-start(bf16[12,16,512]{2,1,0:T(8,128)(2,1)S(1)} %get-tuple-element.121), channel_id=1, source_target_pairs={{1,0},{2,1},{3,2},{4,3},{5,4},{6,5},{7,6},{8,7},{9,8},{10,9},{11,1... | collective-permute-start | bytes 589832 | tf_op jit(solution)/shard_map/ppermute | solution.py:19
  28.2 10.3 %collective-permute-start.4 = (bf16[2,128,512]{2,1,0:T(8,128)(2,1)S(1)}, bf16[2,128,512]{2,1,0:T(8,128)(2,1)S(1)}, u32[]{:S(2)}, u32[]{:S(2)}) collective-permute-start(bf16[2,128,512]{2,1,0:T(8,128)(2,1)S(1)} %pad_maximum_fusion.1), channel_id=1, source_target_pairs={{8,0},{9,1},{10,2},{11,3},{12,4},{13,5},{14,6},{15,7},{0,8},{1,9},... | collective-permute-start | bytes 786440 | tf_op jit(solution)/shard_map/ppermute | solution.py:27
  31.4 7.7 %copy-start.2 = (bf16[3,10,96,3,128]{4,1,3,0,2:T(8,128)(2,1)}, bf16[3,10,96,3,128]{4,1,3,0,2:T(8,128)(2,1)S(1)}, u32[]{:S(2)}) copy-start(bf16[3,10,96,3,128]{4,1,3,0,2:T(8,128)(2,1)S(1)} %convert_bitcast_fusion) | copy-start | bytes 6635524
  44.0 8.0 %copy-start.7 = (bf16[960,512]{1,0:T(8,128)(2,1)}, bf16[960,512]{1,0:T(8,128)(2,1)S(1)}, u32[]{:S(2)}) copy-start(bf16[960,512]{1,0:T(8,128)(2,1)S(1)} %fusion.19) | copy-start | bytes 2949124
  44.0 4.2 %copy-start.13 = (bf16[1024,512]{1,0:T(8,128)(2,1)S(1)}, bf16[1024,512]{1,0:T(8,128)(2,1)}, u32[]{:S(2)}) copy-start(bf16[1024,512]{1,0:T(8,128)(2,1)} %param.28) | copy-start | bytes 3145732
  44.0 4.2 %copy-start.15 = (bf16[10,96,512]{2,1,0:T(8,128)(2,1)S(1)}, bf16[10,96,512]{2,1,0:T(8,128)(2,1)}, u32[]{:S(2)}) copy-start(bf16[10,96,512]{2,1,0:T(8,128)(2,1)} %param.29) | copy-start | bytes 2949124
  48.1 13.2 %copy-start.16 = (bf16[960,1024]{1,0:T(8,128)(2,1)}, bf16[960,1024]{1,0:T(8,128)(2,1)S(1)}, u32[]{:S(2)}) copy-start(bf16[960,1024]{1,0:T(8,128)(2,1)S(1)} %get-tuple-element.124) | copy-start | bytes 5898244
  51.9 6.1 %copy-start.9 = (bf16[960,512]{1,0:T(8,128)(2,1)}, bf16[960,512]{1,0:T(8,128)(2,1)S(1)}, u32[]{:S(2)}) copy-start(bf16[960,512]{1,0:T(8,128)(2,1)S(1)} %add_convert_fusion) | copy-start | bytes 2949124
  75.6 10.1 %collective-permute-start.5 = (bf16[2,128,512]{2,1,0:T(8,128)(2,1)S(1)}, bf16[2,128,512]{2,1,0:T(8,128)(2,1)S(1)}, u32[]{:S(2)}, u32[]{:S(2)}) collective-permute-start(bf16[2,128,512]{2,1,0:T(8,128)(2,1)S(1)} %pad_maximum_fusion.2), channel_id=1, source_target_pairs={{8,0},{9,1},{10,2},{11,3},{12,4},{13,5},{14,6},{15,7},{0,8},{1,9},... | collective-permute-start | bytes 786440 | tf_op jit(solution)/shard_map/ppermute | solution.py:27
  86.2 8.6 %collective-permute-start.6 = (bf16[12,16,512]{2,1,0:T(8,128)(2,1)S(1)}, bf16[12,16,512]{2,1,0:T(8,128)(2,1)S(1)}, u32[]{:S(2)}, u32[]{:S(2)}) collective-permute-start(bf16[12,16,512]{2,1,0:T(8,128)(2,1)S(1)} %get-tuple-element.109), channel_id=1, source_target_pairs={{0,1},{1,2},{2,3},{3,4},{4,5},{5,6},{6,7},{7,8},{8,9},{9,10},{10,1... | collective-permute-start | bytes 589832 | tf_op jit(solution)/shard_map/ppermute | solution.py:18
  86.2 8.6 %collective-permute-start.7 = (bf16[12,16,512]{2,1,0:T(8,128)(2,1)S(1)}, bf16[12,16,512]{2,1,0:T(8,128)(2,1)S(1)}, u32[]{:S(2)}, u32[]{:S(2)}) collective-permute-start(bf16[12,16,512]{2,1,0:T(8,128)(2,1)S(1)} %get-tuple-element.110), channel_id=1, source_target_pairs={{1,0},{2,1},{3,2},{4,3},{5,4},{6,5},{7,6},{8,7},{9,8},{10,9},{11,1... | collective-permute-start | bytes 589832 | tf_op jit(solution)/shard_map/ppermute | solution.py:19
  94.9 5.6 %copy-start.17 = (bf16[960,1024]{1,0:T(8,128)(2,1)S(1)}, bf16[960,1024]{1,0:T(8,128)(2,1)}, u32[]{:S(2)}) copy-start(bf16[960,1024]{1,0:T(8,128)(2,1)} %copy-done.16) | copy-start | bytes 5898244
  95.0 5.5 %copy-start.8 = (bf16[960,512]{1,0:T(8,128)(2,1)S(1)}, bf16[960,512]{1,0:T(8,128)(2,1)}, u32[]{:S(2)}) copy-start(bf16[960,512]{1,0:T(8,128)(2,1)} %copy-done.7) | copy-start | bytes 2949124
  95.0 5.5 %copy-start.14 = (bf16[1024,512]{1,0:T(8,128)(2,1)S(1)}, bf16[1024,512]{1,0:T(8,128)(2,1)}, u32[]{:S(2)}) copy-start(bf16[1024,512]{1,0:T(8,128)(2,1)} %param.28) | copy-start | bytes 3145732
  95.2 7.6 %collective-permute-start.8 = (bf16[1,96,512]{2,1,0:T(8,128)(2,1)S(1)}, bf16[1,96,512]{2,1,0:T(8,128)(2,1)S(1)}, u32[]{:S(2)}, u32[]{:S(2)}) collective-permute-start(bf16[1,96,512]{2,1,0:T(8,128)(2,1)S(1)} %get-tuple-element.118), channel_id=1, source_target_pairs={{0,16},{16,32},{32,48},{48,64},{64,80},{80,96},{96,112},{112,128},... | collective-permute-start | bytes 294920 | tf_op jit(solution)/shard_map/ppermute | solution.py:18
  99.2 7.6 %collective-permute-start.9 = (bf16[1,96,512]{2,1,0:T(8,128)(2,1)S(1)}, bf16[1,96,512]{2,1,0:T(8,128)(2,1)S(1)}, u32[]{:S(2)}, u32[]{:S(2)}) collective-permute-start(bf16[1,96,512]{2,1,0:T(8,128)(2,1)S(1)} %get-tuple-element.119), channel_id=1, source_target_pairs={{16,0},{32,16},{48,32},{64,48},{80,64},{96,80},{112,96},{128,112},... | collective-permute-start | bytes 294920 | tf_op jit(solution)/shard_map/ppermute | solution.py:19
  102.6 4.3 %copy-start.10 = (bf16[960,512]{1,0:T(8,128)(2,1)S(1)}, bf16[960,512]{1,0:T(8,128)(2,1)}, u32[]{:S(2)}) copy-start(bf16[960,512]{1,0:T(8,128)(2,1)} %copy-done.9) | copy-start | bytes 2949124
  351.7 3.6 copy-start.5
  (5 other events, 10.8 us)
Sparse Core Ops, SparseCore 0:
  72.0 279.6 all-reduce.5
where the time goes:
time: 366 us; the launch traced here: 365 us
  waiting for transfers between devices  275 us (75%)
  matrix products  30.9 us (8%)
  starting transfers between devices  23 us (6%)
  between operations  14.5 us (4%)
  other arithmetic  13 us (4%)
  local copies, waits for them, and re-layouts  8.96 us (2%)
    psum x1, waiting for transfers between devices, local(): lax.psum((mix_local, up_local, down_local), ('lat', 'lon'))  243 us
    ppermute x2, waiting for transfers between devices, shifted(): return lax.ppermute(block, axis, route)  15.9 us
    ppermute x4, waiting for transfers between devices, extended_2(): before = lax.ppermute(last, axis, up)  11.6 us
    ppermute x4, starting transfers between devices, extended_2(): after = lax.ppermute(leading, axis, down)  10.9 us
    ppermute x4, starting transfers between devices, extended_2(): before = lax.ppermute(last, axis, up)  8.71 us
  transfers between devices with their start and end apart: 11, of which 7 were waited for; matrix products, arithmetic and copies ran while one was open for 3% of the time, Pallas kernels for 0%

commit v1 on v0

--- a/solution.py
+++ b/solution.py
@@ -149,7 +149,9 @@
         hidden_grad.astype(jnp.float32).reshape(lat_rows, lon_cols, channels) + adjoint
     ).astype(jnp.bfloat16)
     grad_scale = 1.0 / math.sqrt(points * lat_count * lon_count)
-    mix_total, up_total, down_total = lax.psum((mix_local, up_local, down_local), ("lat", "lon"))
+    mix_total, up_total, down_total = lax.psum(
+        lax.psum((mix_local, up_local, down_local), "lon"), "lat"
+    )
     mix_out = (mix_total * grad_scale).astype(jnp.bfloat16)
     up_out = (up_total * grad_scale).astype(jnp.bfloat16)
     down_out = (down_total * grad_scale).astype(jnp.bfloat16)

time: 366 us -> 448 us (1.22)
  waiting for transfers between devices: 275 us -> 366 us
    ppermute x4, waiting for transfers between devices: 11.6 us -> 84.3 us  [extended_2(): before = lax.ppermute(last, axis, up)]
    psum x1 -> x2, waiting for transfers between devices: 243 us -> 264 us  [the longest x1 185 us: local(): lax.psum((mix_local, up_local, down_local), 'lon')]
  transfers between devices with their start and end apart: 11 -> 12, of which waited for: 7 -> 8; matrix products, arithmetic and copies ran while one was open for 3% -> 3% of each run, Pallas kernels for 0% -> 0%
where the time goes in v1:
time: 448 us; the launch traced here: 447 us
  waiting for transfers between devices  366 us (82%)
  matrix products  27.3 us (6%)
  starting transfers between devices  21.8 us (5%)
  between operations  14.5 us (3%)
  other arithmetic  10.5 us (2%)
  local copies, waits for them, and re-layouts  6.95 us (2%)
    psum x1, waiting for transfers between devices, local(): lax.psum((mix_local, up_local, down_local), 'lon')  185 us
    ppermute x4, waiting for transfers between devices, extended_2(): before = lax.ppermute(last, axis, up)  84.3 us
    psum x1, waiting for transfers between devices, local(): lax.psum(lax.psum((mix_local, up_local, down_local), 'lon'), 'lat')  78.1 us
    ppermute x2, waiting for transfers between devices, shifted(): return lax.ppermute(block, axis, route)  14.7 us
    ppermute x4, starting transfers between devices, extended_2(): after = lax.ppermute(leading, axis, down)  10.9 us
  transfers between devices with their start and end apart: 12, of which 8 were waited for; matrix products, arithmetic and copies ran while one was open for 3% of the time, Pallas kernels for 0%

profile of v1, /device:TPU:8, one launch (start us, length us, event | category | flops | bytes accessed | tf_op | source)
XLA Modules:
  0.0 446.8 jit_solution(6971192744813861346)
XLA Ops:
  9.6 4.6 %collective-permute-start = (bf16[1,96,512]{2,1,0:T(8,128)(2,1)S(1)}, bf16[1,96,512]{2,1,0:T(8,128)(2,1)S(1)}, u32[]{:S(2)}, u32[]{:S(2)}) collective-permute-start(bf16[1,96,512]{2,1,0:T(8,128)(2,1)S(1)} %get-tuple-element.126), channel_id=1, source_target_pairs={{0,16},{16,32},{32,48},{48,64},{64,80},{80,96},{96,112},{112,128},... | collective-permute-start | bytes 294920 | tf_op jit(solution)/shard_map/ppermute | solution.py:18
  17.8 4.1 collective-permute-start.3
  22.0 6.0 %collective-permute-done.2 = bf16[12,16,512]{2,1,0:T(8,128)(2,1)S(1)} collective-permute-done((bf16[12,16,512]{2,1,0:T(8,128)(2,1)S(1)}, bf16[12,16,512]{2,1,0:T(8,128)(2,1)S(1)}, u32[]{:S(2)}, u32[]{:S(2)}) %collective-permute-start.2) | collective-permute-done | bytes 196640 | tf_op jit(solution)/shard_map/ppermute | solution.py:18
  28.2 2.1 collective-permute-start.4
  31.4 7.1 %collective-permute-done.4 = bf16[2,128,512]{2,1,0:T(8,128)(2,1)S(1)} collective-permute-done((bf16[2,128,512]{2,1,0:T(8,128)(2,1)S(1)}, bf16[2,128,512]{2,1,0:T(8,128)(2,1)S(1)}, u32[]{:S(2)}, u32[]{:S(2)}) %collective-permute-start.4) | collective-permute-done | bytes 262176 | tf_op jit(solution)/shard_map/ppermute | solution.py:27
  39.1 1.9 fusion.11
  42.2 1.7 fusion.19
  44.0 4.1 multiply_convert_fusion
  48.1 2.3 fusion.5
  51.6 2.6 fusion.46
  54.3 2.6 fusion.47
  56.9 3.6 fusion.22
  60.7 185.5 %all-reduce.8.cloned.1.call-done = (f32[3,512,512]{2,1,0:T(8,128)}, f32[512,1024]{1,0:T(8,128)}, f32[1024,512]{1,0:T(8,128)}) async-done(((f32[3,512,512]{2,1,0:T(8,128)}, f32[512,1024]{1,0:T(8,128)}, f32[1024,512]{1,0:T(8,128)}), (f32[3,512,512]{2,1,0:T(8,128)}, f32[512,1024]{1,0:T(8,128)}, f32[1024,512]{1,0:T(8,128)})) %all-reduce.8.cloned.1.call-update) | async-done | bytes 7340048 | tf_op jit(solution)/shard_map/psum | solution.py:153
  246.2 1.7 convolution_convert_fusion
  248.2 2.3 convolution_bitcast_fusion
  250.5 1.5 slice_bitcast_fusion.2
  253.2 2.5 collective-permute-start.5
  255.7 7.5 %collective-permute-done.5 = bf16[2,128,512]{2,1,0:T(8,128)(2,1)S(1)} collective-permute-done((bf16[2,128,512]{2,1,0:T(8,128)(2,1)S(1)}, bf16[2,128,512]{2,1,0:T(8,128)(2,1)S(1)}, u32[]{:S(2)}, u32[]{:S(2)}) %collective-permute-start.5) | collective-permute-done | bytes 262176 | tf_op jit(solution)/shard_map/ppermute | solution.py:27
  263.8 4.1 collective-permute-start.7
  268.1 76.9 %collective-permute-done.6 = bf16[12,16,512]{2,1,0:T(8,128)(2,1)S(1)} collective-permute-done((bf16[12,16,512]{2,1,0:T(8,128)(2,1)S(1)}, bf16[12,16,512]{2,1,0:T(8,128)(2,1)S(1)}, u32[]{:S(2)}, u32[]{:S(2)}) %collective-permute-start.6) | collective-permute-done | bytes 196640 | tf_op jit(solution)/shard_map/ppermute | solution.py:18
  348.1 2.1 add_convert_fusion.1
  350.4 3.1 collective-permute-done.9
  355.0 78.1 %all-reduce.10.cloned.1.call-done = (f32[3,512,512]{2,1,0:T(8,128)}, f32[512,1024]{1,0:T(8,128)}, f32[1024,512]{1,0:T(8,128)}) async-done(((f32[3,512,512]{2,1,0:T(8,128)}, f32[512,1024]{1,0:T(8,128)}, f32[1024,512]{1,0:T(8,128)}), (f32[3,512,512]{2,1,0:T(8,128)}, f32[512,1024]{1,0:T(8,128)}, f32[1024,512]{1,0:T(8,128)})) %all-reduce.10.cloned.1.call-update) | async-done | bytes 7340048 | tf_op jit(solution)/shard_map/psum | solution.py:152
  433.1 3.6 multiply_convert_fusion.1
  (79 shorter events, 20.6 us)
Async XLA Ops:
  7.2 34.1 %copy-start = (bf16[3,512,512]{2,1,0:T(8,128)(2,1)S(1)}, bf16[3,512,512]{2,1,0:T(8,128)(2,1)}, u32[]{:S(2)}) copy-start(bf16[3,512,512]{2,1,0:T(8,128)(2,1)} %param.26) | copy-start | bytes 4718596
  7.2 14.8 %copy-start.7 = (bf16[3,10,3,33]{3,2,1,0:T(4,128)(2,1)S(1)}, bf16[3,10,3,33]{3,2,1,0:T(4,128)(2,1)}, u32[]{:S(2)}) copy-start(bf16[3,10,3,33]{3,2,1,0:T(4,128)(2,1)} %param.24) | copy-start | bytes 17824
  7.2 239.0 %all-reduce.8.cloned.1.call-start = ((), (), s32[]{:S(2)}) async-start(), calls=%async_computation | async-start | bytes 14680064 | tf_op jit(solution)/shard_map/psum | solution.py:153
  8.3 9.4 %collective-permute-start.1 = (bf16[1,96,512]{2,1,0:T(8,128)(2,1)S(1)}, bf16[1,96,512]{2,1,0:T(8,128)(2,1)S(1)}, u32[]{:S(2)}, u32[]{:S(2)}) collective-permute-start(bf16[1,96,512]{2,1,0:T(8,128)(2,1)S(1)} %get-tuple-element.125), channel_id=1, source_target_pairs={{16,0},{32,16},{48,32},{64,48},{80,64},{96,80},{112,96},{128,112},... | collective-permute-start | bytes 294920 | tf_op jit(solution)/shard_map/ppermute | solution.py:19
  9.6 6.8 %collective-permute-start = (bf16[1,96,512]{2,1,0:T(8,128)(2,1)S(1)}, bf16[1,96,512]{2,1,0:T(8,128)(2,1)S(1)}, u32[]{:S(2)}, u32[]{:S(2)}) collective-permute-start(bf16[1,96,512]{2,1,0:T(8,128)(2,1)S(1)} %get-tuple-element.126), channel_id=1, source_target_pairs={{0,16},{16,32},{32,48},{48,64},{64,80},{80,96},{96,112},{112,128},... | collective-permute-start | bytes 294920 | tf_op jit(solution)/shard_map/ppermute | solution.py:18
  17.7 10.2 %collective-permute-start.2 = (bf16[12,16,512]{2,1,0:T(8,128)(2,1)S(1)}, bf16[12,16,512]{2,1,0:T(8,128)(2,1)S(1)}, u32[]{:S(2)}, u32[]{:S(2)}) collective-permute-start(bf16[12,16,512]{2,1,0:T(8,128)(2,1)S(1)} %get-tuple-element.123), channel_id=1, source_target_pairs={{0,1},{1,2},{2,3},{3,4},{4,5},{5,6},{6,7},{7,8},{8,9},{9,10},{10,1... | collective-permute-start | bytes 589832 | tf_op jit(solution)/shard_map/ppermute | solution.py:18
  17.8 10.2 %collective-permute-start.3 = (bf16[12,16,512]{2,1,0:T(8,128)(2,1)S(1)}, bf16[12,16,512]{2,1,0:T(8,128)(2,1)S(1)}, u32[]{:S(2)}, u32[]{:S(2)}) collective-permute-start(bf16[12,16,512]{2,1,0:T(8,128)(2,1)S(1)} %get-tuple-element.124), channel_id=1, source_target_pairs={{1,0},{2,1},{3,2},{4,3},{5,4},{6,5},{7,6},{8,7},{9,8},{10,9},{11,1... | collective-permute-start | bytes 589832 | tf_op jit(solution)/shard_map/ppermute | solution.py:19
  28.2 10.3 %collective-permute-start.4 = (bf16[2,128,512]{2,1,0:T(8,128)(2,1)S(1)}, bf16[2,128,512]{2,1,0:T(8,128)(2,1)S(1)}, u32[]{:S(2)}, u32[]{:S(2)}) collective-permute-start(bf16[2,128,512]{2,1,0:T(8,128)(2,1)S(1)} %pad_maximum_fusion.1), channel_id=1, source_target_pairs={{8,0},{9,1},{10,2},{11,3},{12,4},{13,5},{14,6},{15,7},{0,8},{1,9},... | collective-permute-start | bytes 786440 | tf_op jit(solution)/shard_map/ppermute | solution.py:27
  31.4 7.7 %copy-start.2 = (bf16[3,10,96,3,128]{4,1,3,0,2:T(8,128)(2,1)}, bf16[3,10,96,3,128]{4,1,3,0,2:T(8,128)(2,1)S(1)}, u32[]{:S(2)}) copy-start(bf16[3,10,96,3,128]{4,1,3,0,2:T(8,128)(2,1)S(1)} %convert_bitcast_fusion) | copy-start | bytes 6635524
  44.0 4.2 copy-start.9
  44.0 4.2 copy-start.11
  48.1 6.1 %copy-start.12 = (bf16[960,1024]{1,0:T(8,128)(2,1)}, bf16[960,1024]{1,0:T(8,128)(2,1)S(1)}, u32[]{:S(2)}) copy-start(bf16[960,1024]{1,0:T(8,128)(2,1)S(1)} %get-tuple-element.127) | copy-start | bytes 5898244
  60.5 372.6 %all-reduce.10.cloned.1.call-start = ((), (), s32[]{:S(2)}) async-start(), calls=%async_computation.1 | async-start | bytes 14680064 | tf_op jit(solution)/shard_map/psum | solution.py:152
  246.2 2.0 copy-start.3
  253.2 10.0 %collective-permute-start.5 = (bf16[2,128,512]{2,1,0:T(8,128)(2,1)S(1)}, bf16[2,128,512]{2,1,0:T(8,128)(2,1)S(1)}, u32[]{:S(2)}, u32[]{:S(2)}) collective-permute-start(bf16[2,128,512]{2,1,0:T(8,128)(2,1)S(1)} %pad_maximum_fusion.2), channel_id=1, source_target_pairs={{8,0},{9,1},{10,2},{11,3},{12,4},{13,5},{14,6},{15,7},{0,8},{1,9},... | collective-permute-start | bytes 786440 | tf_op jit(solution)/shard_map/ppermute | solution.py:27
  263.7 81.3 %collective-permute-start.6 = (bf16[12,16,512]{2,1,0:T(8,128)(2,1)S(1)}, bf16[12,16,512]{2,1,0:T(8,128)(2,1)S(1)}, u32[]{:S(2)}, u32[]{:S(2)}) collective-permute-start(bf16[12,16,512]{2,1,0:T(8,128)(2,1)S(1)} %get-tuple-element.112), channel_id=1, source_target_pairs={{0,1},{1,2},{2,3},{3,4},{4,5},{5,6},{6,7},{7,8},{8,9},{9,10},{10,1... | collective-permute-start | bytes 589832 | tf_op jit(solution)/shard_map/ppermute | solution.py:18
  263.8 81.3 %collective-permute-start.7 = (bf16[12,16,512]{2,1,0:T(8,128)(2,1)S(1)}, bf16[12,16,512]{2,1,0:T(8,128)(2,1)S(1)}, u32[]{:S(2)}, u32[]{:S(2)}) collective-permute-start(bf16[12,16,512]{2,1,0:T(8,128)(2,1)S(1)} %get-tuple-element.113), channel_id=1, source_target_pairs={{1,0},{2,1},{3,2},{4,3},{5,4},{6,5},{7,6},{8,7},{9,8},{10,9},{11,1... | collective-permute-start | bytes 589832 | tf_op jit(solution)/shard_map/ppermute | solution.py:19
  345.2 2.9 copy-start.10
  345.2 2.9 copy-start.13
  345.4 5.0 %collective-permute-start.8 = (bf16[1,96,512]{2,1,0:T(8,128)(2,1)S(1)}, bf16[1,96,512]{2,1,0:T(8,128)(2,1)S(1)}, u32[]{:S(2)}, u32[]{:S(2)}) collective-permute-start(bf16[1,96,512]{2,1,0:T(8,128)(2,1)S(1)} %get-tuple-element.121), channel_id=1, source_target_pairs={{0,16},{16,32},{32,48},{48,64},{64,80},{80,96},{96,112},{112,128},... | collective-permute-start | bytes 294920 | tf_op jit(solution)/shard_map/ppermute | solution.py:18
  346.8 6.7 %collective-permute-start.9 = (bf16[1,96,512]{2,1,0:T(8,128)(2,1)S(1)}, bf16[1,96,512]{2,1,0:T(8,128)(2,1)S(1)}, u32[]{:S(2)}, u32[]{:S(2)}) collective-permute-start(bf16[1,96,512]{2,1,0:T(8,128)(2,1)S(1)} %get-tuple-element.122), channel_id=1, source_target_pairs={{16,0},{32,16},{48,32},{64,48},{80,64},{96,80},{112,96},{128,112},... | collective-permute-start | bytes 294920 | tf_op jit(solution)/shard_map/ppermute | solution.py:19
  433.1 3.6 copy-start.5
  436.7 2.0 copy-start.4
  436.7 3.2 copy-start.1
  (2 other events, 2.9 us)
Sparse Core Ops, SparseCore 0:
  60.6 185.5 all-reduce.7
  249.0 183.9 all-reduce.9
